TPU v7x, 128 devices: a whole 4x4x4 slice. The times are simulated.
128 devices in a mesh: expert: 16 (over z, y), tensor: 8 (over x, core).
Axes of the slice: x: 4, y: 4, z: 4, core: 2. Of those that a mesh axis runs over, the one named last changes fastest.
Arguments:
- layer_input: bfloat16 [4096, 2, 4096], P('expert', None, 'tensor'), may hold values from -6 to 6
- base_input: bfloat16 [4096, 4096], P('expert', 'tensor'), may hold values from -6 to 6
- cotangent: bfloat16 [4096, 4096], P('expert', 'tensor'), may hold values from -6 to 6
- cross_weight: bfloat16 [16, 2, 4096, 4096], P('expert', None, 'tensor'), may hold values from -0.0625 to 0.0625
- cross_bias: float32 [16, 4096], P('expert', 'tensor'), may hold values from -3 to 3
- routes: int32 [4096, 2], P('expert'), may hold values from 0 to 15, as said below
- gate_values: float32 [4096, 2], P('expert'), may hold values from 0.2 to 1
Outputs:
- layer_out: bfloat16 [4096, 4096], P('expert', 'tensor')
- input_grad: bfloat16 [4096, 2, 4096], P('expert', None, 'tensor')
- base_grad: bfloat16 [4096, 4096], P('expert', 'tensor')
- weight_grad: bfloat16 [16, 2, 4096, 4096], P('expert', None, 'tensor')
- bias_grad: float32 [16, 4096], P('expert', 'tensor')
Inputs may be any that keep to these rules, and one draw needn't show every extreme that they name: `routes`: each row names two different experts. Among the 256 rows of one index of expert (aligned blocks), no expert is named more than 48 times, and one expert, the same in every block, is named exactly 48 times in every block.
All inputs are finite; a program needn't handle non-finite values.
Results may differ from a plain program's by a relative error of at most 0.017.
Values may be sent and summed in bfloat16 or wider, within the bound.
A program may use at most 128 MiB of HBM per device.

v0:
```python
import jax
import jax.numpy as jnp
from jax import lax
from jax.sharding import PartitionSpec as P


def route_positions(routes, experts, capacity):
    flat_routes = routes.reshape(-1)
    one_hot = (flat_routes[:, None] == jnp.arange(experts, dtype=jnp.int32)[None, :]).astype(
        jnp.int32
    )
    ranks = jnp.cumsum(one_hot, axis=0) - one_hot
    return flat_routes * capacity + jnp.sum(ranks * one_hot, axis=1)


def per_device(layer_input, base_input, cotangent, cross_weight, cross_bias, routes, gate_values):
    rows = layer_input.shape[0]
    width = layer_input.shape[2]
    full_out = cross_weight.shape[3]
    experts = lax.axis_size("expert")
    capacity = (3 * rows + experts - 1) // experts
    slots_total = experts * capacity
    scale = 1.0 / jnp.sqrt(jnp.float32(2 * rows))
    positions = route_positions(routes, experts, capacity)
    route_inputs = jnp.broadcast_to(layer_input[:, None], (rows, 2, 2, width)).reshape(
        2 * rows, 2, width
    )
    send_inputs = jnp.zeros((slots_total, 2, width), jnp.bfloat16).at[positions].set(route_inputs)
    send_inputs = send_inputs.reshape(experts, capacity, 2, width)
    weighted = (cotangent.astype(jnp.float32) * base_input.astype(jnp.float32)).astype(jnp.bfloat16)
    weighted_rows = lax.all_gather(weighted, "tensor", axis=1, tiled=True)
    cot_width = weighted_rows.shape[1]
    route_cot = (gate_values[:, :, None] * weighted_rows[:, None, :].astype(jnp.float32)).astype(
        jnp.bfloat16
    )
    send_cot = (
        jnp.zeros((slots_total, cot_width), jnp.bfloat16)
        .at[positions]
        .set(route_cot.reshape(2 * rows, cot_width))
    )
    send_cot = send_cot.reshape(experts, capacity, cot_width)
    arrived_inputs, arrived_cot = (
        lax.all_to_all(send_inputs, "expert", split_axis=0, concat_axis=0, tiled=True),
        lax.all_to_all(send_cot, "expert", split_axis=0, concat_axis=0, tiled=True),
    )
    flat_inputs = arrived_inputs.reshape(slots_total, 2 * width)
    flat_weight = cross_weight.reshape(2 * width, full_out)
    partial_value = jnp.dot(flat_inputs, flat_weight, preferred_element_type=jnp.float32)
    summed = lax.psum_scatter(
        partial_value.astype(jnp.bfloat16), "tensor", scatter_dimension=1, tiled=True
    ).astype(jnp.float32)
    cross = (summed + cross_bias).astype(jnp.bfloat16)
    returned = lax.all_to_all(
        cross.reshape(experts, capacity, width), "expert", split_axis=0, concat_axis=0, tiled=True
    )
    cross_routes = (
        returned.reshape(slots_total, width)[positions].reshape(rows, 2, width).astype(jnp.float32)
    )
    mixture = jnp.sum(gate_values[:, :, None] * cross_routes, axis=1)
    gate_total = jnp.sum(gate_values, axis=1)[:, None]
    layer_out = (
        base_input.astype(jnp.float32) * mixture
        + gate_total * layer_input[:, 0, :].astype(jnp.float32)
    ).astype(jnp.bfloat16)
    base_grad = (cotangent.astype(jnp.float32) * mixture).astype(jnp.bfloat16)
    cot_rows = arrived_cot.reshape(slots_total, cot_width)
    weight_sum = lax.dot_general(
        flat_inputs, cot_rows, (((0,), (0,)), ((), ())), preferred_element_type=jnp.float32
    )
    route_grads = lax.dot_general(
        cot_rows, flat_weight, (((1,), (1,)), ((), ())), preferred_element_type=jnp.float32
    )
    own_columns = lax.dynamic_slice_in_dim(cot_rows, lax.axis_index("tensor") * width, width, 1)
    bias_sum = jnp.sum(own_columns.astype(jnp.float32), axis=0)
    weight_grad = (weight_sum * scale).astype(jnp.bfloat16).reshape(1, 2, width, full_out)
    bias_grad = (bias_sum * scale).reshape(1, width)
    route_back = lax.all_to_all(
        route_grads.astype(jnp.bfloat16).reshape(experts, capacity, 2, width),
        "expert",
        split_axis=0,
        concat_axis=0,
        tiled=True,
    )
    picked = (
        route_back.reshape(slots_total, 2, width)[positions]
        .reshape(rows, 2, 2, width)
        .astype(jnp.float32)
    )
    grad_sum = jnp.sum(picked, axis=1)
    grad_sum = grad_sum.at[:, 0, :].add(gate_total * cotangent.astype(jnp.float32))
    input_grad = grad_sum.astype(jnp.bfloat16)
    return (layer_out, input_grad, base_grad, weight_grad, bias_grad)


def solution(mesh):
    in_specs = (
        P("expert", None, "tensor"),
        P("expert", "tensor"),
        P("expert", "tensor"),
        P("expert", None, "tensor", None),
        P("expert", "tensor"),
        P("expert", None),
        P("expert", None),
    )
    out_specs = (
        P("expert", "tensor"),
        P("expert", None, "tensor"),
        P("expert", "tensor"),
        P("expert", None, "tensor", None),
        P("expert", "tensor"),
    )
    return jax.shard_map(
        per_device, mesh=mesh, in_specs=in_specs, out_specs=out_specs, check_vma=False
    )
```

profile of v0, /device:TPU:0, one launch (start us, length us, event | category | flops | bytes accessed | tf_op | source)
XLA Modules:
  0.0 356.7 jit_solution(16559496350380601480)
XLA Ops:
  7.2 0.0 reduce-scatter.2.cloned.1.call-start
  7.2 0.7 broadcast_multiply_fusion.1
  7.9 0.8 copy.32
  8.7 0.1 eq.29
  8.9 0.1 eq.25
  9.0 0.1 copy.31
  9.1 0.1 mul.96
  9.3 1.2 reduce-window.6
  10.5 0.2 slice_reduce_fusion
  10.7 0.1 fusion.9
  10.8 1.6 broadcast_in_dim.7
  12.4 0.8 broadcast_in_dim.6
  13.2 13.8 %scatter_fusion = bf16[768,2,512]{2,1,0:T(2,128)(2,1)S(1)} fusion(bf16[768,2,512]{2,1,0:T(2,128)(2,1)S(1)} %broadcast_in_dim.6, s32[512]{0:T(512)S(1)} %bitcast.61, bf16[512,2,512]{2,1,0:T(2,128)(2,1)S(1)} %bitcast.57), kind=kCustom, calls=%fused_computation.2 | custom fusion | bytes 3147776 | tf_op jit(solution)/shard_map/scatter | solution.py:28
  27.1 30.7 %all_to_all.20 = bf16[16,48,2,512]{3,2,1,0:T(2,128)(2,1)S(1)} all-to-all(bf16[16,48,2,512]{3,2,1,0:T(2,128)(2,1)S(1)} %bitcast.54), channel_id=1, replica_groups=mesh['expert'=16,'tensor'=8] {'expert'}, dimensions={0} | all-to-all | bytes 3145728 | tf_op jit(solution)/shard_map/all_to_all | solution.py:43
  57.8 0.4 copy.39
  58.2 0.0 copy-start.1
  58.2 1.2 copy-done.1
  59.5 11.9 %convolution_convert_fusion = bf16[768,4096]{1,0:T(8,128)(2,1)} fusion(bf16[768,1024]{1,0:T(8,128)(2,1)S(1)} %bitcast.59, bf16[1024,4096]{1,0:T(8,128)(2,1)} %bitcast.67), kind=kOutput, calls=%fused_computation.6 | convolution fusion | flops 6445596672 | bytes 16252928 | tf_op jit(solution)/shard_map/dot_general | solution.py:48
  71.4 0.0 copy-start.5
  71.4 0.0 copy-start.4
  71.4 0.0 reduce-scatter.2.cloned.1.call-update
  71.4 0.0 copy-start
  71.4 0.0 copy-start.2
  71.4 0.0 copy-start.3
  71.4 40.0 %reduce-scatter.2.cloned.1.call-done = bf16[768,512]{1,0:T(8,128)(2,1)} async-done(((bf16[768,4096]{1,0:T(8,128)(2,1)}), bf16[768,512]{1,0:T(8,128)(2,1)}) %reduce-scatter.2.cloned.1.call-update) | async-done | bytes 786448 | tf_op jit(solution)/shard_map/reduce_scatter | solution.py:49
  111.5 0.0 copy-done.5
  111.5 2.2 add_convert_fusion
  113.6 7.0 %all-to-all-start.1 = ((bf16[16,48,512]{2,1,0:T(8,128)(2,1)}), bf16[16,48,512]{2,1,0:T(8,128)(2,1)S(1)}, u32[]{:S(2)}, u32[]{:S(2)}) async-start(bf16[16,48,512]{2,1,0:T(8,128)(2,1)} %bitcast.7), calls=%async_computation.2 | async-start | bytes 1572864 | tf_op jit(solution)/shard_map/all_to_all | solution.py:53
  120.6 0.2 all-gather.2.cloned.1.call-start
  120.8 0.0 copy-done.4
  120.9 0.1 copy.30
  121.0 13.4 %all-to-all-done.1 = bf16[16,48,512]{2,1,0:T(8,128)(2,1)S(1)} async-done(((bf16[16,48,512]{2,1,0:T(8,128)(2,1)}), bf16[16,48,512]{2,1,0:T(8,128)(2,1)S(1)}, u32[]{:S(2)}, u32[]{:S(2)}) %all-to-all-start.1) | async-done | bytes 786464 | tf_op jit(solution)/shard_map/all_to_all | solution.py:53
  134.4 2.0 gather_fusion
  136.4 0.7 reshape.161
  137.1 1.3 multiply_reduce_fusion
  138.4 0.0 copy-done
  138.4 0.0 copy-done.2
  138.4 0.0 copy-done.3
  138.4 1.1 fusion.6
  139.5 0.0 all-gather.2.cloned.1.call-update
  139.5 0.1 mul.102
  139.7 22.7 %all-gather.2.cloned.1.call-done = bf16[256,4096]{1,0:T(8,128)(2,1)} async-done(((bf16[256,512]{1,0:T(8,128)(2,1)}), bf16[256,4096]{1,0:T(8,128)(2,1)}) %all-gather.2.cloned.1.call-update) | async-done | bytes 2097168 | tf_op jit(solution)/shard_map/all_gather | solution.py:31
  162.4 8.2 %mul.105 = f32[256,2,4096]{2,1,0:T(2,128)} broadcast(bf16[256,4096]{1,0:T(8,128)(2,1)} %all-gather.2.cloned.1.call-done), dimensions={0,2} | broadcast | bytes 10485760 | tf_op jit(solution)/shard_map/mul | solution.py:33
  170.6 10.9 %mul.106 = f32[512,4096]{1,0:T(8,128)} reshape(f32[256,2,4096]{2,1,0:T(2,128)} %mul.105) | data formatting | bytes 16777216 | tf_op jit(solution)/shard_map/mul | solution.py:33
  181.5 12.7 %scatter_custom_fusion.1 = bf16[768,4096]{1,0:T(8,128)(2,1)} fusion(s32[512]{0:T(512)S(1)} %bitcast.63, f32[512,4096]{1,0:T(8,128)} %mul.106, f32[512]{0:T(512)S(1)} %mul.102, bf16[]{:T(256)} %constant.44.clone.1), kind=kCustom, calls=%fused_computation.7 | custom fusion | flops 4194304 | bytes 14682114 | tf_op jit(solution)/shard_map/scatter | solution.py:39
  194.2 7.0 %all-to-all-start.2 = ((bf16[16,48,4096]{2,1,0:T(8,128)(2,1)}), bf16[16,48,4096]{2,1,0:T(8,128)(2,1)}, u32[]{:S(2)}, u32[]{:S(2)}) async-start(bf16[16,48,4096]{2,1,0:T(8,128)(2,1)} %bitcast.53), calls=%async_computation.3 | async-start | bytes 12582912 | tf_op jit(solution)/shard_map/all_to_all | solution.py:44
  201.2 94.4 %all-to-all-done.2 = bf16[16,48,4096]{2,1,0:T(8,128)(2,1)} async-done(((bf16[16,48,4096]{2,1,0:T(8,128)(2,1)}), bf16[16,48,4096]{2,1,0:T(8,128)(2,1)}, u32[]{:S(2)}, u32[]{:S(2)}) %all-to-all-start.2) | async-done | bytes 6291488 | tf_op jit(solution)/shard_map/all_to_all | solution.py:44
  295.7 11.0 %convolution_convert_fusion.1 = bf16[768,1024]{1,0:T(8,128)(2,1)S(1)} fusion(bf16[768,4096]{1,0:T(8,128)(2,1)} %bitcast.11, bf16[1024,4096]{1,0:T(8,128)(2,1)} %bitcast.68), kind=kOutput, calls=%fused_computation.11 | convolution fusion | flops 6443237376 | bytes 16252928 | tf_op jit(solution)/shard_map/dot_general | solution.py:70
  306.6 1.3 convert_reduce_fusion.1
  307.9 2.4 reshape.157
  310.3 5.0 %all-to-all-start.3 = ((bf16[16,48,2,512]{3,2,1,0:T(2,128)(2,1)}), bf16[16,48,2,512]{3,2,1,0:T(2,128)(2,1)S(1)}, u32[]{:S(2)}, u32[]{:S(2)}) async-start(bf16[16,48,2,512]{3,2,1,0:T(2,128)(2,1)} %reshape.157), calls=%async_computation.4 | async-start | bytes 3145728 | tf_op jit(solution)/shard_map/all_to_all | solution.py:77
  315.3 0.6 broadcast_multiply_fusion
  315.9 11.4 %multiply_convert_fusion = bf16[1024,4096]{1,0:T(8,128)(2,1)} fusion(bf16[768,1024]{1,0:T(8,128)(2,1)} %bitcast.60, bf16[768,4096]{1,0:T(8,128)(2,1)} %bitcast.11), kind=kOutput, calls=%fused_computation.4 | convolution fusion | flops 6450839552 | bytes 16252928 | tf_op jit(solution)/shard_map/dot_general | solution.py:67
  327.2 11.3 %all-to-all-done.3 = bf16[16,48,2,512]{3,2,1,0:T(2,128)(2,1)S(1)} async-done(((bf16[16,48,2,512]{3,2,1,0:T(2,128)(2,1)}), bf16[16,48,2,512]{3,2,1,0:T(2,128)(2,1)S(1)}, u32[]{:S(2)}, u32[]{:S(2)}) %all-to-all-start.3) | async-done | bytes 1572896 | tf_op jit(solution)/shard_map/all_to_all | solution.py:77
  338.5 3.6 gather_fusion.1
  342.1 1.4 convert_reduce_fusion
  343.5 0.5 slice_add_fusion
  344.0 4.7 %scatter-add.4 = f32[256,2,512]{2,1,0:T(2,128)S(1)} dynamic-update-slice(f32[256,2,512]{2,1,0:T(2,128)S(1)} %convert_reduce_fusion, f32[256,1,512]{2,1,0:T(1,128)S(1)} %slice_add_fusion, s32[]{:T(128)} %constant.46.clone.1, s32[]{:T(128)} %constant.46.clone.1, s32[]{:T(128)} %constant.46.clone.1) | dynamic-update-slice | bytes 1048580 | tf_op jit(solution)/shard_map/scatter-add | solution.py:90
  348.8 1.2 convert_element_type.90
  (6 shorter events, 0.1 us)
Async XLA Ops:
  7.2 104.3 %reduce-scatter.2.cloned.1.call-start = ((), (), s32[]{:S(2)}) async-start(), calls=%async_computation.5 | async-start | bytes 7077888 | tf_op jit(solution)/shard_map/reduce_scatter | solution.py:49
  58.2 1.2 copy-start.1
  71.4 40.1 %copy-start.5 = (f32[1,512]{1,0:T(1,128)S(1)}, f32[1,512]{1,0:T(1,128)}, u32[]{:S(2)}) copy-start(f32[1,512]{1,0:T(1,128)} %param.13) | copy-start | bytes 6148
  71.4 49.5 %copy-start.4 = (f32[256,2]{0,1:T(2,128)S(1)}, f32[256,2]{0,1:T(2,128)}, u32[]{:S(2)}) copy-start(f32[256,2]{0,1:T(2,128)} %param.15) | copy-start | bytes 6148
  71.4 67.0 %copy-start = (bf16[256,2,512]{2,1,0:T(2,128)(2,1)S(1)}, bf16[256,2,512]{2,1,0:T(2,128)(2,1)}, u32[]{:S(2)}) copy-start(bf16[256,2,512]{2,1,0:T(2,128)(2,1)} %param.9) | copy-start | bytes 1572868
  71.4 67.0 %copy-start.2 = (bf16[256,512]{1,0:T(8,128)(2,1)S(1)}, bf16[256,512]{1,0:T(8,128)(2,1)}, u32[]{:S(2)}) copy-start(bf16[256,512]{1,0:T(8,128)(2,1)} %param.11) | copy-start | bytes 786436
  71.4 67.0 %copy-start.3 = (bf16[256,512]{1,0:T(8,128)(2,1)S(1)}, bf16[256,512]{1,0:T(8,128)(2,1)}, u32[]{:S(2)}) copy-start(bf16[256,512]{1,0:T(8,128)(2,1)} %param.10) | copy-start | bytes 786436
  113.6 20.8 %all-to-all-start.1 = ((bf16[16,48,512]{2,1,0:T(8,128)(2,1)}), bf16[16,48,512]{2,1,0:T(8,128)(2,1)S(1)}, u32[]{:S(2)}, u32[]{:S(2)}) async-start(bf16[16,48,512]{2,1,0:T(8,128)(2,1)} %bitcast.7), calls=%async_computation.2 | async-start | bytes 1572864 | tf_op jit(solution)/shard_map/all_to_all | solution.py:53
  120.6 41.8 %all-gather.2.cloned.1.call-start = ((), (), s32[]{:S(2)}) async-start(), calls=%async_computation.6 | async-start | bytes 2359296 | tf_op jit(solution)/shard_map/all_gather | solution.py:31
  194.2 101.5 %all-to-all-start.2 = ((bf16[16,48,4096]{2,1,0:T(8,128)(2,1)}), bf16[16,48,4096]{2,1,0:T(8,128)(2,1)}, u32[]{:S(2)}, u32[]{:S(2)}) async-start(bf16[16,48,4096]{2,1,0:T(8,128)(2,1)} %bitcast.53), calls=%async_computation.3 | async-start | bytes 12582912 | tf_op jit(solution)/shard_map/all_to_all | solution.py:44
  310.3 28.2 %all-to-all-start.3 = ((bf16[16,48,2,512]{3,2,1,0:T(2,128)(2,1)}), bf16[16,48,2,512]{3,2,1,0:T(2,128)(2,1)S(1)}, u32[]{:S(2)}, u32[]{:S(2)}) async-start(bf16[16,48,2,512]{3,2,1,0:T(2,128)(2,1)} %reshape.157), calls=%async_computation.4 | async-start | bytes 3145728 | tf_op jit(solution)/shard_map/all_to_all | solution.py:77
Sparse Core Ops, SparseCore 0:
  71.5 39.9 reduce-scatter.1
  139.6 22.7 all-gather.1
where the time goes:
time: 358 us; the launch traced here: 357 us
  waiting for transfers between devices  182 us (51%)
  local copies, waits for them, and re-layouts  52 us (15%)
  matrix products  34.2 us (10%)
  blocking collectives  30.7 us (9%)
  other arithmetic  24.3 us (7%)
  starting transfers between devices  19.2 us (5%)
  between operations  14.3 us (4%)
    all_to_all x1, waiting for transfers between devices, per_device(): lax.all_to_all(send_cot, 'expert', split_axis=0, concat_axis=0, tiled=True)  94.4 us
    reduce_scatter x1, waiting for transfers between devices, per_device(): lax.psum_scatter(partial_value.astype(jnp.bfloat16), 'tensor', scatter_di...  40 us
    all_to_all x1, blocking collectives, per_device(): lax.all_to_all(send_inputs, 'expert', split_axis=0, concat_axis=0, tiled=...  30.7 us
    all_gather x1, waiting for transfers between devices, per_device(): weighted_rows = lax.all_gather(weighted, 'tensor', axis=1, tiled=True)  22.7 us
    mul x3, local copies, waits for them, and re-layouts, per_device(): gate_values[:, :, None] * weighted_rows[:, None, :].astype(jnp.float32)  19.2 us
    scatter x1, local copies, waits for them, and re-layouts, per_device(): jnp.zeros((slots_total, 2, width), jnp.bfloat16).at[positions]  13.8 us
    all_to_all x1, waiting for transfers between devices, per_device(): lax.all_to_all(cross.reshape(experts, capacity, width), 'expert', split_a...  13.4 us
    scatter x1, other arithmetic, per_device(): send_cot = jnp.zeros((slots_total, cot_width), jnp.bfloat16).at[positions...  12.7 us
  transfers between devices with their start and end apart: 5, of which 5 were waited for; matrix products, arithmetic and copies ran while one was open for 3% of the time, Pallas kernels for 0%

commit v1 on v0

v1 whole, which is shorter than its diff:
```python
import functools

import jax
import jax.numpy as jnp
from jax import lax
from jax.experimental import pallas as pl
from jax.experimental.pallas import tpu as pltpu
from jax.sharding import PartitionSpec as P

MESH = pl.DeviceIdType.MESH
F32 = jnp.float32
BF16 = jnp.bfloat16
NN = (((1,), (0,)), ((), ()))
TN = (((0,), (0,)), ((), ()))
NT = (((1,), (1,)), ((), ()))


def dot(a, b, dims=NN):
    return lax.dot_general(a, b, dims, preferred_element_type=F32)


def kernel(
    sizes,
    x_ref, base_ref, cot_ref, w_ref, bias_ref, routes_ref, gates_ref,
    layer_out, input_grad, base_grad, weight_grad, bias_grad,
    pick, send_c, send_x, xa, xt, ca, wv, part_send, part_recv, own, far_send, far_recv,
    near_send, near_recv, cross_send, cross_back, grad_acc, grad_send, grad_back, wg,
    w_sem, wg_sem, c_ss, c_rs, x_ss, x_rs, ag_ss, ag_rs, p_ss, p_rs, far_ss, far_rs,
    near_ss, near_rs, g_ss, g_rs, y_ss, y_rs,
):
    experts, rows, width, cap = sizes
    slots = experts * cap
    feats = 2 * width
    half = experts // 2
    me = lax.axis_index("expert")
    tensor = lax.axis_index("tensor")
    chip, core = tensor // 2, lax.rem(tensor, 2)
    other = 1 - core

    def at(step, which):
        return lax.rem(chip + step, 4) * 2 + which

    own_t, left_t, right_t, far_t = at(0, core), at(3, core), at(1, core), at(2, core)
    partner = at(0, other)

    def peer(d):
        return lax.rem(me + d, experts)

    barrier = pltpu.get_barrier_semaphore()

    def greet(d, carry):
        pl.semaphore_signal(barrier, inc=1, device_id={"expert": peer(d)}, device_id_type=MESH)
        return carry

    lax.fori_loop(1, experts, greet, 0)
    for t in (partner, left_t, right_t):
        pl.semaphore_signal(barrier, inc=1, device_id={"tensor": t}, device_id_type=MESH)

    def w_copy(t):
        return pltpu.make_async_copy(
            w_ref.at[:, pl.ds(pl.multiple_of(t * width, width), width)], wv.at[t], w_sem.at[t]
        )

    def start_w(t, carry):
        w_copy(t).start()
        return carry

    lax.fori_loop(0, 8, start_w, 0)

    below = (
        lax.broadcasted_iota(jnp.int32, (rows, rows), 1)
        < lax.broadcasted_iota(jnp.int32, (rows, rows), 0)
    ).astype(F32).astype(BF16)
    expert_id = lax.broadcasted_iota(jnp.int32, (rows, experts), 1)
    first = expert_id.astype(F32) * float(cap)
    slot_id = lax.broadcasted_iota(jnp.int32, (rows, slots), 1).astype(F32)
    routes = routes_ref[...]
    gates = gates_ref[...]
    weighted = (cot_ref[...].astype(F32) * base_ref[...].astype(F32)).astype(BF16).astype(F32)
    sent = None
    for k in range(2):
        named = (routes[:, k : k + 1] == expert_id).astype(F32)
        place = first + dot(below, named.astype(BF16))
        if k == 0:
            first = first + jnp.sum(named, axis=0, keepdims=True)
        position = jnp.sum(named * place, axis=1, keepdims=True)
        chosen = (slot_id == position).astype(F32).astype(BF16)
        pick[k] = chosen
        route_cot = (gates[:, k : k + 1] * weighted).astype(BF16)
        piece = dot(chosen, route_cot, TN)
        sent = piece if sent is None else sent + piece
    send_c[...] = sent.astype(BF16).reshape(experts, cap, width)

    def over(src, dst, ss, rs, d):
        return pltpu.make_async_remote_copy(
            src_ref=src.at[peer(d)], dst_ref=dst.at[me], send_sem=ss.at[d], recv_sem=rs.at[me],
            device_id={"expert": peer(d)}, device_id_type=MESH,
        )

    def exchange(src, dst, ss, rs):
        def body(d, carry):
            over(src, dst, ss, rs, d).start()
            return carry

        lax.fori_loop(1, experts, body, 0)

    def landed(dst, ss, rs):
        def body(d, carry):
            source = peer(d)
            pltpu.make_async_remote_copy(
                src_ref=dst.at[source], dst_ref=dst.at[source], send_sem=ss.at[d],
                recv_sem=rs.at[source], device_id={"expert": source}, device_id_type=MESH,
            ).wait_recv()
            return carry

        lax.fori_loop(1, experts, body, 0)

    def drain(src, dst, ss, rs):
        def body(d, carry):
            over(src, dst, ss, rs, d).wait_send()
            return carry

        lax.fori_loop(1, experts, body, 0)

    pl.semaphore_wait(barrier, experts + 2)
    ca_own = ca.at[own_t]
    exchange(send_c, ca_own, c_ss, c_rs)
    send_x[...] = dot(pick[0] + pick[1], x_ref[...], TN).astype(BF16).reshape(experts, cap, feats)
    exchange(send_x, xa, x_ss, x_rs)
    ca[own_t, me] = send_c[me]
    xa[me] = send_x[me]

    def wait_w(t, carry):
        w_copy(t).wait()
        return carry

    lax.fori_loop(0, 8, wait_w, 0)

    low, high, whole = pl.ds(0, half), pl.ds(half, half), pl.ds(0, experts)
    moves = [
        (own_t, low, right_t, left_t),
        (own_t, high, right_t, left_t),
        (own_t, high, left_t, right_t),
        (own_t, low, left_t, right_t),
        (own_t, whole, partner, partner),
        (left_t, low, right_t, far_t),
        (right_t, high, left_t, far_t),
        (left_t, whole, partner, at(3, other)),
        (right_t, whole, partner, at(1, other)),
        (far_t, whole, partner, at(2, other)),
    ]

    def move(i):
        block, part, target, _ = moves[i]
        region = ca.at[block, part]
        return pltpu.make_async_remote_copy(
            src_ref=region, dst_ref=region, send_sem=ag_ss.at[i], recv_sem=ag_rs.at[i],
            device_id={"tensor": target}, device_id_type=MESH,
        )

    def arrived(i):
        _, part, _, block = moves[i]
        region = ca.at[block, part]
        pltpu.make_async_remote_copy(
            src_ref=region, dst_ref=region, send_sem=ag_ss.at[i], recv_sem=ag_rs.at[i],
            device_id={"tensor": partner}, device_id_type=MESH,
        ).wait_recv()

    landed(ca_own, c_ss, c_rs)
    for i in (0, 2, 1, 3, 4):
        move(i).start()

    def cot_block(t):
        return ca[t].reshape(slots, width)

    def grads_of(t):
        return dot(cot_block(t), wv[t], NT)

    scale = 1.0 / (2.0 * rows) ** 0.5
    bias_grad[...] = jnp.sum(cot_block(own_t).astype(F32), axis=0, keepdims=True) * scale
    grad_acc[...] = grads_of(own_t)
    arrived(4)
    grad_acc[...] += grads_of(partner)
    arrived(0)
    move(5).start()
    arrived(2)
    move(6).start()
    arrived(1)
    move(7).start()
    arrived(3)
    move(8).start()
    landed(xa, x_ss, x_rs)

    def partial(t):
        return dot(xa[...].reshape(slots, feats), wv[t])

    def pair(k):
        return pltpu.make_async_remote_copy(
            src_ref=part_send.at[k], dst_ref=part_recv.at[k], send_sem=p_ss.at[k],
            recv_sem=p_rs.at[k], device_id={"tensor": partner}, device_id_type=MESH,
        )

    def to_partner(i, carry):
        k = lax.rem(i + 2, 4)
        part_send[k] = partial(at(k, other)).astype(BF16)
        pair(k).start()
        return carry

    lax.fori_loop(0, 4, to_partner, 0)

    middle = slots // 2

    def far(i):
        target = (right_t, left_t)[i]
        return pltpu.make_async_remote_copy(
            src_ref=far_send.at[i], dst_ref=far_recv.at[i], send_sem=far_ss.at[i],
            recv_sem=far_rs.at[i], device_id={"tensor": target}, device_id_type=MESH,
        )

    def near(i):
        target = (right_t, left_t)[i]
        return pltpu.make_async_remote_copy(
            src_ref=near_send.at[i], dst_ref=near_recv.at[i], send_sem=near_ss.at[i],
            recv_sem=near_rs.at[i], device_id={"tensor": target}, device_id_type=MESH,
        )

    mine = partial(at(2, core))
    pair(2).wait_recv()
    far_send[...] = (mine + part_recv[2].astype(F32)).astype(BF16).reshape(2, middle, width)
    far(0).start()
    far(1).start()

    def chip_sum(i, carry):
        k = lax.rem(2 * i + 1, 5)
        own[i] = partial(at(k, core))
        pair(k).wait_recv()
        own[i] += part_recv[k].astype(F32)
        return carry

    lax.fori_loop(0, 3, chip_sum, 0)

    def add_grads(t):
        grad_acc[...] += grads_of(t)

    add_grads(left_t)
    add_grads(right_t)
    arrived(5)
    arrived(6)
    move(9).start()
    arrived(7)
    add_grads(at(3, other))
    arrived(8)
    add_grads(at(1, other))
    add_grads(far_t)
    arrived(9)
    grad_send[...] = (
        (grad_acc[...] + grads_of(at(2, other))).astype(BF16).reshape(experts, cap, feats)
    )
    exchange(grad_send, grad_back, g_ss, g_rs)
    grad_back[me] = grad_send[me]

    for i in range(2):
        far(i).wait_recv()
        rest = pl.ds(i * middle, middle)
        keep = pl.ds((1 - i) * middle, middle)
        near_send[i, rest] = (own[i, rest] + far_recv[i].astype(F32)).astype(BF16)
        near_send[i, keep] = own[i, keep].astype(BF16)
        near(i).start()

    xt[...] = xa[...].reshape(slots, feats).T

    def wg_copy(t, slot):
        return pltpu.make_async_copy(
            wg.at[slot],
            weight_grad.at[:, pl.ds(pl.multiple_of(t * width, width), width)],
            wg_sem.at[slot],
        )

    def weight_block(t, carry):
        slot = lax.rem(t, 2)

        @pl.when(t >= 2)
        def _():
            wg_copy(t - 2, slot).wait()

        wg[slot] = (dot(xt[...], cot_block(t)) * scale).astype(BF16)
        wg_copy(t, slot).start()
        return carry

    lax.fori_loop(0, 8, weight_block, 0)

    near(0).wait_recv()
    near(1).wait_recv()
    cross = own[2] + near_recv[0].astype(F32) + near_recv[1].astype(F32) + bias_ref[...]
    cross_send[...] = cross.astype(BF16).reshape(experts, cap, width)
    exchange(cross_send, cross_back, y_ss, y_rs)
    cross_back[me] = cross_send[me]

    gate0, gate1 = gates_ref[:, 0:1], gates_ref[:, 1:2]
    gate_total = gate0 + gate1
    cot = cot_ref[...].astype(F32)
    landed(grad_back, g_ss, g_rs)
    grad_sum = dot(pick[0] + pick[1], grad_back[...].reshape(slots, feats))
    input_grad[:, :width] = (grad_sum[:, :width] + gate_total * cot).astype(BF16)
    input_grad[:, width:] = grad_sum[:, width:].astype(BF16)

    landed(cross_back, y_ss, y_rs)
    back = cross_back[...].reshape(slots, width)
    mixture = gate0 * dot(pick[0], back) + gate1 * dot(pick[1], back)
    layer_out[...] = (
        base_ref[...].astype(F32) * mixture + gate_total * x_ref[:, :width].astype(F32)
    ).astype(BF16)
    base_grad[...] = (cot * mixture).astype(BF16)

    wg_copy(6, 0).wait()
    wg_copy(7, 1).wait()
    drain(send_c, ca_own, c_ss, c_rs)
    drain(send_x, xa, x_ss, x_rs)
    for i in range(10):
        move(i).wait_send()
    for k in range(4):
        pair(k).wait_send()
    for i in range(2):
        far(i).wait_send()
        near(i).wait_send()
    drain(grad_send, grad_back, g_ss, g_rs)
    drain(cross_send, cross_back, y_ss, y_rs)


def per_device(layer_input, base_input, cotangent, cross_weight, cross_bias, routes, gate_values):
    rows, _, width = layer_input.shape
    full_out = cross_weight.shape[3]
    experts = lax.axis_size("expert")
    cap = (3 * rows + experts - 1) // experts
    slots, feats = experts * cap, 2 * width
    vmem = pl.BlockSpec(memory_space=pltpu.VMEM)
    hbm = pl.BlockSpec(memory_space=pl.ANY)
    dma = pltpu.SemaphoreType.DMA
    layer_out, input_grad, base_grad, weight_grad, bias_grad = pl.pallas_call(
        functools.partial(kernel, (experts, rows, width, cap)),
        out_shape=(
            jax.ShapeDtypeStruct((rows, width), BF16),
            jax.ShapeDtypeStruct((rows, feats), BF16),
            jax.ShapeDtypeStruct((rows, width), BF16),
            jax.ShapeDtypeStruct((feats, full_out), BF16),
            jax.ShapeDtypeStruct((1, width), F32),
        ),
        in_specs=[vmem, vmem, vmem, hbm, vmem, vmem, vmem],
        out_specs=(vmem, vmem, vmem, hbm, vmem),
        scratch_shapes=[
            pltpu.VMEM((2, rows, slots), BF16),
            pltpu.VMEM((experts, cap, width), BF16),
            pltpu.VMEM((experts, cap, feats), BF16),
            pltpu.VMEM((experts, cap, feats), BF16),
            pltpu.VMEM((feats, slots), BF16),
            pltpu.VMEM((8, experts, cap, width), BF16),
            pltpu.VMEM((8, feats, width), BF16),
            pltpu.VMEM((4, slots, width), BF16),
            pltpu.VMEM((4, slots, width), BF16),
            pltpu.VMEM((3, slots, width), F32),
            pltpu.VMEM((2, slots // 2, width), BF16),
            pltpu.VMEM((2, slots // 2, width), BF16),
            pltpu.VMEM((2, slots, width), BF16),
            pltpu.VMEM((2, slots, width), BF16),
            pltpu.VMEM((experts, cap, width), BF16),
            pltpu.VMEM((experts, cap, width), BF16),
            pltpu.VMEM((slots, feats), F32),
            pltpu.VMEM((experts, cap, feats), BF16),
            pltpu.VMEM((experts, cap, feats), BF16),
            pltpu.VMEM((2, feats, width), BF16),
            dma((8,)), dma((2,)),
            dma((experts,)), dma((experts,)), dma((experts,)), dma((experts,)),
            dma((10,)), dma((10,)), dma((4,)), dma((4,)), dma((2,)), dma((2,)),
            dma((2,)), dma((2,)),
            dma((experts,)), dma((experts,)), dma((experts,)), dma((experts,)),
        ],
        compiler_params=pltpu.CompilerParams(
            collective_id=0, has_side_effects=True, vmem_limit_bytes=62 * 1024 * 1024
        ),
        name="cross_experts",
    )(
        layer_input.reshape(rows, feats), base_input, cotangent,
        cross_weight.reshape(feats, full_out), cross_bias, routes, gate_values,
    )
    return (
        layer_out,
        input_grad.reshape(rows, 2, width),
        base_grad,
        weight_grad.reshape(1, 2, width, full_out),
        bias_grad,
    )


def solution(mesh):
    in_specs = (
        P("expert", None, "tensor"),
        P("expert", "tensor"),
        P("expert", "tensor"),
        P("expert", None, "tensor", None),
        P("expert", "tensor"),
        P("expert", None),
        P("expert", None),
    )
    out_specs = (
        P("expert", "tensor"),
        P("expert", None, "tensor"),
        P("expert", "tensor"),
        P("expert", None, "tensor", None),
        P("expert", "tensor"),
    )
    return jax.shard_map(
        per_device, mesh=mesh, in_specs=in_specs, out_specs=out_specs, check_vma=False
    )
```

time: 358 us -> 116 us (0.32)
  waiting for transfers between devices: 182 us -> 0 us
  Pallas kernels: 0 us -> 96.1 us
  matrix products: 34.2 us -> 0 us
  local copies, waits for them, and re-layouts: 52 us -> 18.9 us
  blocking collectives: 30.7 us -> 0 us
  other arithmetic: 24.3 us -> 0 us
  starting transfers between devices: 19.2 us -> 0 us
  between operations: 14.3 us -> 0.64 us
    all_to_all x3 -> x0, waiting for transfers between devices: 119 us -> none  [the longest x1 94.4 us: per_device(): lax.all_to_all(send_cot, 'expert', split_axis=0, concat_axis=0, tiled=True)]
    pallas_call x0 -> x1, Pallas kernels: none -> 96.1 us  [per_device(): pl.pallas_call(functools.partial(kernel, (experts, rows, width, cap)), ou...]
    reduce_scatter x1 -> x0, waiting for transfers between devices: 40 us -> none  [per_device(): lax.psum_scatter(partial_value.astype(jnp.bfloat16), 'tensor', scatter_di...]
    dot_general x3 -> x0, matrix products: 34.2 us -> none  [the longest x1 11.9 us: per_device(): jnp.dot(flat_inputs, flat_weight, preferred_element_type=jnp.float32)]
    all_to_all x1 -> x0, blocking collectives: 30.7 us -> none  [per_device(): lax.all_to_all(send_inputs, 'expert', split_axis=0, concat_axis=0, tiled=...]
    all_gather x1 -> x0, waiting for transfers between devices: 22.7 us -> none  [per_device(): weighted_rows = lax.all_gather(weighted, 'tensor', axis=1, tiled=True)]
    mul x5 -> x0, local copies, waits for them, and re-layouts: 19.5 us -> none  [the longest x3 19.2 us: per_device(): gate_values[:, :, None] * weighted_rows[:, None, :].astype(jnp.float32)]
    all_to_all x3 -> x0, starting transfers between devices: 19 us -> none  [the longest x1 7.02 us: per_device(): lax.all_to_all(send_cot, 'expert', split_axis=0, concat_axis=0, tiled=True)]
  transfers between devices with their start and end apart: 5 -> 0, of which waited for: 5 -> 0; matrix products, arithmetic and copies ran while one was open for 3% -> 0% of each run, Pallas kernels for 0% -> 0%
where the time goes in v1:
time: 116 us
  Pallas kernels  96.1 us (83%)
  local copies, waits for them, and re-layouts  18.9 us (16%)
    pallas_call x1, Pallas kernels, per_device(): pl.pallas_call(functools.partial(kernel, (experts, rows, width, cap)), ou...  96.1 us
    unnamed x9, local copies, waits for them, and re-layouts  16.7 us

profile of v1, /device:TPU:0, one launch (start us, length us, event | category | flops | bytes accessed | tf_op | source)
XLA Modules:
  0.0 115.6 jit_solution(15609505330654861489)
XLA Ops:
  0.6 1.5 %copy.12.routes_ref = s32[256,2]{1,0:T(8,128)} copy(s32[256,2]{0,1:T(2,128)} %param.12) | data formatting | bytes 4096 | tf_op args[5]
  2.1 1.5 %copy.13.gates_ref = f32[256,2]{1,0:T(8,128)} copy(f32[256,2]{0,1:T(2,128)} %param.13) | data formatting | bytes 4096 | tf_op args[6]
  3.6 1.9 %copy.14 = bf16[32,8,2,512]{3,1,2,0:T(8,128)(2,1)} copy(bf16[32,8,2,512]{3,2,1,0:T(2,128)(2,1)} %bitcast.7) | data formatting | bytes 1048576
  5.5 96.1 %cross_experts.1 = (bf16[256,512]{1,0:T(8,128)(2,1)}, bf16[256,1024]{1,0:T(8,128)(2,1)}, bf16[256,512]{1,0:T(8,128)(2,1)}, bf16[1024,4096]{1,0:T(8,128)(2,1)}, f32[1,512]{1,0:T(1,128)}) custom-call(bf16[256,1024]{1,0:T(8,128)(2,1)} %bitcast.6, bf16[256,512]{1,0:T(8,128)(2,1)} %base_ref.1, bf16[256,512]{1,0:T(8,128)(2,1)} %cot_ref.1, ...), custom_call_target="tpu_custom_call" | custom-call | tf_op jit(solution)/shard_map/cross_experts/pallas_call | solution.py:339
  101.6 2.2 %reshape.24 = bf16[256,2,512]{2,1,0:T(2,128)(2,1)} reshape(bf16[256,1024]{1,0:T(8,128)(2,1)} %get-tuple-element.11) | data formatting | bytes 1048576 | tf_op jit(solution)/shard_map/reshape | solution.py:387
  103.8 1.7 %copy.19 = bf16[256,512]{1,0:T(8,128)(2,1)} copy(bf16[256,512]{1,0:T(8,128)(2,1)} %get-tuple-element.20) | data formatting | bytes 524288
  105.5 1.7 %copy.20 = bf16[256,512]{1,0:T(8,128)(2,1)} copy(bf16[256,512]{1,0:T(8,128)(2,1)} %get-tuple-element.22) | data formatting | bytes 524288
  107.1 0.0 copy-start
  107.2 7.9 %copy.21 = bf16[1,2,512,4096]{3,2,1,0:T(8,128)(2,1)} copy(bf16[1,2,512,4096]{3,2,1,0:T(8,128)(2,1)} %bitcast.5) | data formatting | bytes 16777216
  115.0 0.0 copy-done
  115.0 0.6 copy.22
Async XLA Ops:
  107.1 7.9 %copy-start = (f32[1,512]{1,0:T(1,128)S(1)}, f32[1,512]{1,0:T(1,128)}, u32[]{:S(2)}) copy-start(f32[1,512]{1,0:T(1,128)} %get-tuple-element.24) | copy-start | bytes 6148

commit v2 on v1

v2 whole, which is shorter than its diff:
```python
import functools

import jax
import jax.numpy as jnp
from jax import lax
from jax.experimental import pallas as pl
from jax.experimental.pallas import tpu as pltpu
from jax.sharding import PartitionSpec as P

MESH = pl.DeviceIdType.MESH
F32 = jnp.float32
BF16 = jnp.bfloat16
CHUNKS = 3
NN = (((1,), (0,)), ((), ()))
TN = (((0,), (0,)), ((), ()))
NT = (((1,), (1,)), ((), ()))


def dot(a, b, dims=NN):
    return lax.dot_general(a, b, dims, preferred_element_type=F32)


def kernel(
    sizes,
    x_ref, base_ref, cot_ref, w_ref, bias_ref, routes_ref, gates_ref,
    layer_out, input_grad, base_grad, weight_grad, bias_grad,
    pick, gate_cols, send_c, send_x, xa, xt, ca, wv, part_send, part_recv, own,
    far_send, far_recv, near_send, near_recv, cross_send, cross_back,
    grad_acc, grad_send, grad_back, wg,
    w_sem, wg_sem, c_ss, c_rs, x_ss, x_rs, ag_ss, ag_rs, p_ss, p_rs, far_ss, far_rs,
    near_ss, near_rs, g_ss, g_rs, y_ss, y_rs,
):
    experts, rows, width, lot = sizes
    lot_slots = experts * lot
    slots = CHUNKS * lot_slots
    feats = 2 * width
    half = experts // 2
    middle = half * lot
    me = lax.axis_index("expert")
    tensor = lax.axis_index("tensor")
    chip, core = tensor // 2, lax.rem(tensor, 2)
    other = 1 - core

    def at(step, which):
        return lax.rem(chip + step, 4) * 2 + which

    own_t, left_t, right_t, far_t = at(0, core), at(3, core), at(1, core), at(2, core)
    partner = at(0, other)

    def peer(d):
        return lax.rem(me + d, experts)

    def loop(start, stop, step):
        def run(i, carry):
            step(i)
            return carry

        lax.fori_loop(start, stop, run, 0)

    barrier = pltpu.get_barrier_semaphore()

    def greet(d):
        pl.semaphore_signal(barrier, inc=1, device_id={"expert": peer(d)}, device_id_type=MESH)

    loop(1, experts, greet)
    for t in (partner, left_t, right_t):
        pl.semaphore_signal(barrier, inc=1, device_id={"tensor": t}, device_id_type=MESH)

    def w_copy(t):
        return pltpu.make_async_copy(
            w_ref.at[:, pl.ds(pl.multiple_of(t * width, width), width)], wv.at[t], w_sem.at[t]
        )

    loop(0, 8, lambda t: w_copy(t).start())

    below = (
        lax.broadcasted_iota(jnp.int32, (rows, rows), 1)
        < lax.broadcasted_iota(jnp.int32, (rows, rows), 0)
    ).astype(F32).astype(BF16)
    expert_id = lax.broadcasted_iota(jnp.int32, (rows, experts), 1).astype(F32)
    slot_id = lax.broadcasted_iota(jnp.int32, (rows, slots), 1).astype(F32)
    columns = jnp.concatenate(
        [routes_ref[...].astype(F32), gates_ref[...], jnp.zeros((4, rows), F32)], axis=0
    ).T
    gate_cols[...] = columns
    weighted = (cot_ref[...].astype(F32) * base_ref[...].astype(F32)).astype(BF16).astype(F32)
    sent, before = None, 0.0
    for k in range(2):
        named = (columns[:, k : k + 1] == expert_id).astype(F32)
        place = jnp.sum(
            named * (before + dot(below, named.astype(BF16))), axis=1, keepdims=True
        )
        if k == 0:
            before = jnp.sum(named, axis=0, keepdims=True)
        position = place + float(lot) * jnp.sum(named * expert_id, axis=1, keepdims=True)
        for q in range(1, CHUNKS):
            position += float(lot_slots - lot) * (place >= float(q * lot)).astype(F32)
        chosen = (slot_id == position).astype(F32).astype(BF16)
        pick[k] = chosen
        route_cot = (columns[:, k + 2 : k + 3] * weighted).astype(BF16)
        piece = dot(chosen, route_cot, TN)
        sent = piece if sent is None else sent + piece
    send_c[...] = sent.astype(BF16).reshape(CHUNKS, experts, lot, width)

    def over(src, dst, ss, rs, q, d):
        return pltpu.make_async_remote_copy(
            src_ref=src.at[q, peer(d)], dst_ref=dst.at[q, me], send_sem=ss.at[q, d],
            recv_sem=rs.at[q, me], device_id={"expert": peer(d)}, device_id_type=MESH,
        )

    def exchange(src, dst, ss, rs, q):
        loop(1, experts, lambda d: over(src, dst, ss, rs, q, d).start())

    def landed(dst, ss, rs, q):
        def take(d):
            source = peer(d)
            pltpu.make_async_remote_copy(
                src_ref=dst.at[q, source], dst_ref=dst.at[q, source], send_sem=ss.at[q, d],
                recv_sem=rs.at[q, source], device_id={"expert": source}, device_id_type=MESH,
            ).wait_recv()

        loop(1, experts, take)

    def drain(src, dst, ss, rs):
        for q in range(CHUNKS):
            loop(1, experts, lambda d, q=q: over(src, dst, ss, rs, q, d).wait_send())

    pl.semaphore_wait(barrier, experts + 2)
    ca_own = ca.at[own_t]
    for q in range(CHUNKS):
        exchange(send_c, ca_own, c_ss, c_rs, q)
    send_x[...] = (
        dot(pick[0] + pick[1], x_ref[...], TN).astype(BF16).reshape(CHUNKS, experts, lot, feats)
    )
    for q in range(CHUNKS):
        exchange(send_x, xa, x_ss, x_rs, q)
        ca[own_t, q, me] = send_c[q, me]
        xa[q, me] = send_x[q, me]

    low, high, whole = pl.ds(0, half), pl.ds(half, half), pl.ds(0, experts)
    moves = [
        (own_t, low, right_t, left_t),
        (own_t, high, right_t, left_t),
        (own_t, high, left_t, right_t),
        (own_t, low, left_t, right_t),
        (own_t, whole, partner, partner),
        (left_t, low, right_t, far_t),
        (right_t, high, left_t, far_t),
        (left_t, whole, partner, at(3, other)),
        (right_t, whole, partner, at(1, other)),
        (far_t, whole, partner, at(2, other)),
    ]

    def move(i, q):
        block, part, target, _ = moves[i]
        region = ca.at[block, q, part]
        return pltpu.make_async_remote_copy(
            src_ref=region, dst_ref=region, send_sem=ag_ss.at[i, q], recv_sem=ag_rs.at[i, q],
            device_id={"tensor": target}, device_id_type=MESH,
        )

    def arrived(i, q):
        _, part, _, block = moves[i]
        region = ca.at[block, q, part]
        pltpu.make_async_remote_copy(
            src_ref=region, dst_ref=region, send_sem=ag_ss.at[i, q], recv_sem=ag_rs.at[i, q],
            device_id={"tensor": partner}, device_id_type=MESH,
        ).wait_recv()

    def arrived_all(i):
        for q in range(CHUNKS):
            arrived(i, q)

    for q in range(CHUNKS):
        landed(ca_own, c_ss, c_rs, q)
        for i in (0, 2, 1, 3, 4):
            move(i, q).start()

    def cot_block(t):
        return ca[t].reshape(slots, width)

    def grads_of(t):
        return dot(cot_block(t), wv[t], NT)

    def add_grads(t):
        grad_acc[...] += grads_of(t)

    def pass_on(q):
        arrived(0, q)
        move(5, q).start()
        arrived(2, q)
        move(6, q).start()
        arrived(1, q)
        move(7, q).start()
        arrived(3, q)
        move(8, q).start()

    def partial(t, q):
        return dot(xa[q].reshape(lot_slots, feats), wv[t])

    def pair(k, q):
        return pltpu.make_async_remote_copy(
            src_ref=part_send.at[k, q], dst_ref=part_recv.at[k, q], send_sem=p_ss.at[k, q],
            recv_sem=p_rs.at[k, q], device_id={"tensor": partner}, device_id_type=MESH,
        )

    def ring(send, recv, ss, rs, i, q):
        return pltpu.make_async_remote_copy(
            src_ref=send.at[i, q], dst_ref=recv.at[i, q], send_sem=ss.at[i, q],
            recv_sem=rs.at[i, q], device_id={"tensor": (right_t, left_t)[i]},
            device_id_type=MESH,
        )

    def far(i, q):
        return ring(far_send, far_recv, far_ss, far_rs, i, q)

    def near(i, q):
        return ring(near_send, near_recv, near_ss, near_rs, i, q)

    def to_partner(k, q):
        part_send[k, q] = partial(at(k, other), q).astype(BF16)
        pair(k, q).start()

    def to_far(q):
        mine = partial(far_t, q)
        pair(2, q).wait_recv()
        total = (mine + part_recv[2, q].astype(F32)).astype(BF16)
        far_send[0, q] = total[:middle]
        far_send[1, q] = total[middle:]
        far(0, q).start()
        far(1, q).start()

    def chip_sum(i, k, q):
        mine = partial(at(k, core), q)
        pair(k, q).wait_recv()
        own[i, q] = mine + part_recv[k, q].astype(F32)

    def to_near(q):
        for i in range(2):
            far(i, q).wait_recv()
            rest, keep = pl.ds(i * middle, middle), pl.ds((1 - i) * middle, middle)
            near_send[i, q, rest] = (own[i, q, rest] + far_recv[i, q].astype(F32)).astype(BF16)
            near_send[i, q, keep] = own[i, q, keep].astype(BF16)
            near(i, q).start()

    def to_rows(q):
        near(0, q).wait_recv()
        near(1, q).wait_recv()
        cross = own[2, q] + near_recv[0, q].astype(F32) + near_recv[1, q].astype(F32)
        cross = (cross + bias_ref[...]).astype(BF16)
        cross_send[q] = cross.reshape(experts, lot, width)
        exchange(cross_send, cross_back, y_ss, y_rs, q)
        cross_back[q, me] = cross_send[q, me]

    scale = 1.0 / (2.0 * rows) ** 0.5
    bias_grad[...] = jnp.sum(cot_block(own_t).astype(F32), axis=0, keepdims=True) * scale
    loop(0, 8, lambda t: w_copy(t).wait())
    grad_acc[...] = grads_of(own_t)
    pass_on(0)
    arrived_all(4)
    add_grads(partner)
    pass_on(1)
    landed(xa, x_ss, x_rs, 0)
    to_partner(2, 0)
    pass_on(2)
    landed(xa, x_ss, x_rs, 1)
    to_partner(2, 1)
    to_far(0)
    add_grads(left_t)
    add_grads(right_t)
    landed(xa, x_ss, x_rs, 2)
    to_partner(2, 2)
    to_far(1)
    to_far(2)
    arrived_all(7)
    add_grads(at(3, other))
    arrived_all(8)
    add_grads(at(1, other))
    for q in range(CHUNKS):
        arrived(5, q)
        arrived(6, q)
        move(9, q).start()
    add_grads(far_t)
    loop(0, 2 * CHUNKS, lambda n: to_partner(1 + 2 * lax.rem(n, 2), n // 2))
    arrived_all(9)
    grad_send[...] = (
        (grad_acc[...] + grads_of(at(2, other)))
        .astype(BF16)
        .reshape(CHUNKS, experts, lot, feats)
    )
    for q in range(CHUNKS):
        exchange(grad_send, grad_back, g_ss, g_rs, q)
        grad_back[q, me] = grad_send[q, me]
    loop(0, 2 * CHUNKS, lambda n: chip_sum(lax.rem(n, 2), 1 + 2 * lax.rem(n, 2), n // 2))
    loop(0, CHUNKS, to_near)
    loop(0, CHUNKS, lambda q: to_partner(0, q))
    loop(0, CHUNKS, lambda q: chip_sum(2, 0, q))

    xt[...] = xa[...].reshape(slots, feats).T

    def wg_copy(t, slot):
        return pltpu.make_async_copy(
            wg.at[slot],
            weight_grad.at[:, pl.ds(pl.multiple_of(t * width, width), width)],
            wg_sem.at[slot],
        )

    def weight_block(t):
        slot = lax.rem(t, 2)

        @pl.when(t >= 2)
        def _():
            wg_copy(t - 2, slot).wait()

        wg[slot] = (dot(xt[...], cot_block(t)) * scale).astype(BF16)
        wg_copy(t, slot).start()

    loop(0, 4, weight_block)
    to_rows(0)
    loop(4, 6, weight_block)
    to_rows(1)
    loop(6, 8, weight_block)
    to_rows(2)

    gate0, gate1 = gate_cols[:, 2:3], gate_cols[:, 3:4]
    gate_total = gate0 + gate1
    cot = cot_ref[...].astype(F32)
    for q in range(CHUNKS):
        landed(grad_back, g_ss, g_rs, q)
    grad_sum = dot(pick[0] + pick[1], grad_back[...].reshape(slots, feats))
    input_grad[:, :width] = (grad_sum[:, :width] + gate_total * cot).astype(BF16)
    input_grad[:, width:] = grad_sum[:, width:].astype(BF16)

    for q in range(CHUNKS):
        landed(cross_back, y_ss, y_rs, q)
    back = cross_back[...].reshape(slots, width)
    mixture = gate0 * dot(pick[0], back) + gate1 * dot(pick[1], back)
    layer_out[...] = (
        base_ref[...].astype(F32) * mixture + gate_total * x_ref[:, :width].astype(F32)
    ).astype(BF16)
    base_grad[...] = (cot * mixture).astype(BF16)

    wg_copy(6, 0).wait()
    wg_copy(7, 1).wait()
    drain(send_c, ca_own, c_ss, c_rs)
    drain(send_x, xa, x_ss, x_rs)
    for q in range(CHUNKS):
        for i in range(10):
            move(i, q).wait_send()
        for k in range(4):
            pair(k, q).wait_send()
        for i in range(2):
            far(i, q).wait_send()
            near(i, q).wait_send()
    drain(grad_send, grad_back, g_ss, g_rs)
    drain(cross_send, cross_back, y_ss, y_rs)


def per_device(layer_input, base_input, cotangent, cross_weight, cross_bias, routes, gate_values):
    rows, _, width = layer_input.shape
    full_out = cross_weight.shape[3]
    experts = lax.axis_size("expert")
    cap = (3 * rows + experts - 1) // experts
    lot = cap // CHUNKS
    slots, feats = experts * cap, 2 * width
    vmem = pl.BlockSpec(memory_space=pltpu.VMEM)
    hbm = pl.BlockSpec(memory_space=pl.ANY)
    dma = pltpu.SemaphoreType.DMA

    def routed(features):
        return [pltpu.VMEM((CHUNKS, experts, lot, features), BF16)]

    def pairs(*shape):
        return [dma(shape), dma(shape)]

    layer_out, input_grad, base_grad, weight_grad, bias_grad = pl.pallas_call(
        functools.partial(kernel, (experts, rows, width, lot)),
        out_shape=(
            jax.ShapeDtypeStruct((rows, width), BF16),
            jax.ShapeDtypeStruct((rows, feats), BF16),
            jax.ShapeDtypeStruct((rows, width), BF16),
            jax.ShapeDtypeStruct((feats, full_out), BF16),
            jax.ShapeDtypeStruct((1, width), F32),
        ),
        in_specs=[vmem, vmem, vmem, hbm, vmem, vmem, vmem],
        out_specs=(vmem, vmem, vmem, hbm, vmem),
        scratch_shapes=[
            pltpu.VMEM((2, rows, slots), BF16),
            pltpu.VMEM((rows, 8), F32),
            *routed(width), *routed(feats), *routed(feats),
            pltpu.VMEM((feats, slots), BF16),
            pltpu.VMEM((8, CHUNKS, experts, lot, width), BF16),
            pltpu.VMEM((8, feats, width), BF16),
            pltpu.VMEM((4, CHUNKS, experts * lot, width), BF16),
            pltpu.VMEM((4, CHUNKS, experts * lot, width), BF16),
            pltpu.VMEM((3, CHUNKS, experts * lot, width), F32),
            pltpu.VMEM((2, CHUNKS, experts // 2 * lot, width), BF16),
            pltpu.VMEM((2, CHUNKS, experts // 2 * lot, width), BF16),
            pltpu.VMEM((2, CHUNKS, experts * lot, width), BF16),
            pltpu.VMEM((2, CHUNKS, experts * lot, width), BF16),
            *routed(width), *routed(width),
            pltpu.VMEM((slots, feats), F32),
            *routed(feats), *routed(feats),
            pltpu.VMEM((2, feats, width), BF16),
            dma((8,)), dma((2,)),
            *pairs(CHUNKS, experts), *pairs(CHUNKS, experts),
            *pairs(10, CHUNKS), *pairs(4, CHUNKS), *pairs(2, CHUNKS), *pairs(2, CHUNKS),
            *pairs(CHUNKS, experts), *pairs(CHUNKS, experts),
        ],
        compiler_params=pltpu.CompilerParams(
            collective_id=0, has_side_effects=True, vmem_limit_bytes=62 * 1024 * 1024
        ),
        name="cross_experts",
    )(
        layer_input.reshape(rows, feats), base_input, cotangent,
        cross_weight.reshape(feats, full_out), cross_bias, routes.T, gate_values.T,
    )
    return (
        layer_out,
        input_grad.reshape(rows, 2, width),
        base_grad,
        weight_grad.reshape(1, 2, width, full_out),
        bias_grad,
    )


def solution(mesh):
    in_specs = (
        P("expert", None, "tensor"),
        P("expert", "tensor"),
        P("expert", "tensor"),
        P("expert", None, "tensor", None),
        P("expert", "tensor"),
        P("expert", None),
        P("expert", None),
    )
    out_specs = (
        P("expert", "tensor"),
        P("expert", None, "tensor"),
        P("expert", "tensor"),
        P("expert", None, "tensor", None),
        P("expert", "tensor"),
    )
    return jax.shard_map(
        per_device, mesh=mesh, in_specs=in_specs, out_specs=out_specs, check_vma=False
    )
```

time: 116 us -> 101 us (0.87)
  Pallas kernels: 96.1 us -> 84.1 us
  local copies, waits for them, and re-layouts: 18.9 us -> 15.9 us
    pallas_call x1, Pallas kernels: 96.1 us -> 84.1 us  [per_device(): pl.pallas_call(functools.partial(kernel, (experts, rows, width, lot)), ou...]
    unnamed x9 -> x7, local copies, waits for them, and re-layouts: 16.7 us -> 13.7 us
where the time goes in v2:
time: 101 us
  Pallas kernels  84.1 us (83%)
  local copies, waits for them, and re-layouts  15.9 us (16%)
    pallas_call x1, Pallas kernels, per_device(): pl.pallas_call(functools.partial(kernel, (experts, rows, width, lot)), ou...  84.1 us
    unnamed x7, local copies, waits for them, and re-layouts  13.7 us
    reshape x1, local copies, waits for them, and re-layouts, per_device(): input_grad.reshape(rows, 2, width)  2.22 us

profile of v2, /device:TPU:0, one launch (start us, length us, event | category | flops | bytes accessed | tf_op | source)
XLA Modules:
  0.0 100.7 jit_solution(3923401664963955084)
XLA Ops:
  0.6 1.9 %copy.12 = bf16[32,8,2,512]{3,1,2,0:T(8,128)(2,1)} copy(bf16[32,8,2,512]{3,2,1,0:T(2,128)(2,1)} %bitcast.9) | data formatting | bytes 1048576
  2.5 84.1 %cross_experts.1 = (bf16[256,512]{1,0:T(8,128)(2,1)}, bf16[256,1024]{1,0:T(8,128)(2,1)}, bf16[256,512]{1,0:T(8,128)(2,1)}, bf16[1024,4096]{1,0:T(8,128)(2,1)}, f32[1,512]{1,0:T(1,128)}) custom-call(bf16[256,1024]{1,0:T(8,128)(2,1)} %bitcast.8, bf16[256,512]{1,0:T(8,128)(2,1)} %base_ref.1, bf16[256,512]{1,0:T(8,128)(2,1)} %cot_ref.1, ...), custom_call_target="tpu_custom_call" | custom-call | tf_op jit(solution)/shard_map/cross_experts/pallas_call | solution.py:376
  86.7 2.2 %reshape.24 = bf16[256,2,512]{2,1,0:T(2,128)(2,1)} reshape(bf16[256,1024]{1,0:T(8,128)(2,1)} %get-tuple-element.11) | data formatting | bytes 1048576 | tf_op jit(solution)/shard_map/reshape | solution.py:420
  88.9 1.7 %copy.17 = bf16[256,512]{1,0:T(8,128)(2,1)} copy(bf16[256,512]{1,0:T(8,128)(2,1)} %get-tuple-element.20) | data formatting | bytes 524288
  90.6 1.7 %copy.18 = bf16[256,512]{1,0:T(8,128)(2,1)} copy(bf16[256,512]{1,0:T(8,128)(2,1)} %get-tuple-element.22) | data formatting | bytes 524288
  92.3 0.0 copy-start
  92.3 7.9 %copy.19 = bf16[1,2,512,4096]{3,2,1,0:T(8,128)(2,1)} copy(bf16[1,2,512,4096]{3,2,1,0:T(8,128)(2,1)} %bitcast.7) | data formatting | bytes 16777216
  100.1 0.0 copy-done
  100.1 0.6 copy.20
Async XLA Ops:
  92.3 7.9 %copy-start = (f32[1,512]{1,0:T(1,128)S(1)}, f32[1,512]{1,0:T(1,128)}, u32[]{:S(2)}) copy-start(f32[1,512]{1,0:T(1,128)} %get-tuple-element.24) | copy-start | bytes 6148

commit v3 on v2

--- a/solution.py
+++ b/solution.py
@@ -26,8 +26,8 @@
     layer_out, input_grad, base_grad, weight_grad, bias_grad,
     pick, gate_cols, send_c, send_x, xa, xt, ca, wv, part_send, part_recv, own,
     far_send, far_recv, near_send, near_recv, cross_send, cross_back,
-    grad_acc, grad_send, grad_back, wg,
-    w_sem, wg_sem, c_ss, c_rs, x_ss, x_rs, ag_ss, ag_rs, p_ss, p_rs, far_ss, far_rs,
+    grad_acc, grad_send, grad_back,
+    w_sem, c_ss, c_rs, x_ss, x_rs, ag_ss, ag_rs, p_ss, p_rs, far_ss, far_rs,
     near_ss, near_rs, g_ss, g_rs, y_ss, y_rs,
 ):
     experts, rows, width, lot = sizes
@@ -129,9 +129,10 @@
     ca_own = ca.at[own_t]
     for q in range(CHUNKS):
         exchange(send_c, ca_own, c_ss, c_rs, q)
-    send_x[...] = (
-        dot(pick[0] + pick[1], x_ref[...], TN).astype(BF16).reshape(CHUNKS, experts, lot, feats)
-    )
+    both = pick[0] + pick[1]
+    for p in range(2):
+        sent = dot(both, x_ref[:, p, :], TN).astype(BF16)
+        send_x[:, :, :, p * width : (p + 1) * width] = sent.reshape(CHUNKS, experts, lot, width)
     for q in range(CHUNKS):
         exchange(send_x, xa, x_ss, x_rs, q)
         ca[own_t, q, me] = send_c[q, me]
@@ -298,22 +299,9 @@
 
     xt[...] = xa[...].reshape(slots, feats).T
 
-    def wg_copy(t, slot):
-        return pltpu.make_async_copy(
-            wg.at[slot],
-            weight_grad.at[:, pl.ds(pl.multiple_of(t * width, width), width)],
-            wg_sem.at[slot],
-        )
-
     def weight_block(t):
-        slot = lax.rem(t, 2)
-
-        @pl.when(t >= 2)
-        def _():
-            wg_copy(t - 2, slot).wait()
-
-        wg[slot] = (dot(xt[...], cot_block(t)) * scale).astype(BF16)
-        wg_copy(t, slot).start()
+        columns = pl.ds(pl.multiple_of(t * width, width), width)
+        weight_grad[:, columns] = (dot(xt[...], cot_block(t)) * scale).astype(BF16)
 
     loop(0, 4, weight_block)
     to_rows(0)
@@ -328,20 +316,18 @@
     for q in range(CHUNKS):
         landed(grad_back, g_ss, g_rs, q)
     grad_sum = dot(pick[0] + pick[1], grad_back[...].reshape(slots, feats))
-    input_grad[:, :width] = (grad_sum[:, :width] + gate_total * cot).astype(BF16)
-    input_grad[:, width:] = grad_sum[:, width:].astype(BF16)
+    input_grad[:, 0, :] = (grad_sum[:, :width] + gate_total * cot).astype(BF16)
+    input_grad[:, 1, :] = grad_sum[:, width:].astype(BF16)
 
     for q in range(CHUNKS):
         landed(cross_back, y_ss, y_rs, q)
     back = cross_back[...].reshape(slots, width)
     mixture = gate0 * dot(pick[0], back) + gate1 * dot(pick[1], back)
     layer_out[...] = (
-        base_ref[...].astype(F32) * mixture + gate_total * x_ref[:, :width].astype(F32)
+        base_ref[...].astype(F32) * mixture + gate_total * x_ref[:, 0, :].astype(F32)
     ).astype(BF16)
     base_grad[...] = (cot * mixture).astype(BF16)
 
-    wg_copy(6, 0).wait()
-    wg_copy(7, 1).wait()
     drain(send_c, ca_own, c_ss, c_rs)
     drain(send_x, xa, x_ss, x_rs)
     for q in range(CHUNKS):
@@ -354,6 +340,14 @@
             near(i, q).wait_send()
     drain(grad_send, grad_back, g_ss, g_rs)
     drain(cross_send, cross_back, y_ss, y_rs)
+
+
+def store(*refs):
+    copies = [pltpu.make_async_copy(refs[i], refs[5 + i], refs[10].at[i]) for i in range(5)]
+    for copy in copies:
+        copy.start()
+    for copy in copies:
+        copy.wait()
 
 
 def per_device(layer_input, base_input, cotangent, cross_weight, cross_bias, routes, gate_values):
@@ -373,17 +367,17 @@
     def pairs(*shape):
         return [dma(shape), dma(shape)]
 
-    layer_out, input_grad, base_grad, weight_grad, bias_grad = pl.pallas_call(
+    results = pl.pallas_call(
         functools.partial(kernel, (experts, rows, width, lot)),
         out_shape=(
-            jax.ShapeDtypeStruct((rows, width), BF16),
-            jax.ShapeDtypeStruct((rows, feats), BF16),
-            jax.ShapeDtypeStruct((rows, width), BF16),
-            jax.ShapeDtypeStruct((feats, full_out), BF16),
-            jax.ShapeDtypeStruct((1, width), F32),
+            pltpu.VMEM((rows, width), BF16),
+            pltpu.VMEM((rows, 2, width), BF16),
+            pltpu.VMEM((rows, width), BF16),
+            pltpu.VMEM((feats, full_out), BF16),
+            pltpu.VMEM((1, width), F32),
         ),
         in_specs=[vmem, vmem, vmem, hbm, vmem, vmem, vmem],
-        out_specs=(vmem, vmem, vmem, hbm, vmem),
+        out_specs=(vmem, vmem, vmem, vmem, vmem),
         scratch_shapes=[
             pltpu.VMEM((2, rows, slots), BF16),
             pltpu.VMEM((rows, 8), F32),
@@ -401,23 +395,31 @@
             *routed(width), *routed(width),
             pltpu.VMEM((slots, feats), F32),
             *routed(feats), *routed(feats),
-            pltpu.VMEM((2, feats, width), BF16),
-            dma((8,)), dma((2,)),
+            dma((8,)),
             *pairs(CHUNKS, experts), *pairs(CHUNKS, experts),
             *pairs(10, CHUNKS), *pairs(4, CHUNKS), *pairs(2, CHUNKS), *pairs(2, CHUNKS),
             *pairs(CHUNKS, experts), *pairs(CHUNKS, experts),
         ],
         compiler_params=pltpu.CompilerParams(
-            collective_id=0, has_side_effects=True, vmem_limit_bytes=62 * 1024 * 1024
+            collective_id=0, has_side_effects=True, vmem_limit_bytes=52 * 1024 * 1024
         ),
         name="cross_experts",
     )(
-        layer_input.reshape(rows, feats), base_input, cotangent,
+        layer_input, base_input, cotangent,
         cross_weight.reshape(feats, full_out), cross_bias, routes.T, gate_values.T,
     )
+    layer_out, input_grad, base_grad, weight_grad, bias_grad = pl.pallas_call(
+        store,
+        out_shape=tuple(jax.ShapeDtypeStruct(r.shape, r.dtype) for r in results),
+        in_specs=[hbm] * 5,
+        out_specs=(hbm,) * 5,
+        scratch_shapes=[dma((5,))],
+        compiler_params=pltpu.CompilerParams(vmem_limit_bytes=1024 * 1024),
+        name="store",
+    )(*results)
     return (
         layer_out,
-        input_grad.reshape(rows, 2, width),
+        input_grad,
         base_grad,
         weight_grad.reshape(1, 2, width, full_out),
         bias_grad,

time: 101 us -> 87.9 us (0.87)
  local copies, waits for them, and re-layouts: 15.9 us -> 0 us
  Pallas kernels: 84.1 us -> 86.9 us
    unnamed x7 -> x0, local copies, waits for them, and re-layouts: 13.7 us -> none
    pallas_call x0 -> x1, Pallas kernels: none -> 3.79 us  [per_device(): pl.pallas_call(store, out_shape=tuple((jax.ShapeDtypeStruct(r.shape, r.dt...]
    reshape x1 -> x0, local copies, waits for them, and re-layouts: 2.22 us -> none  [per_device(): input_grad.reshape(rows, 2, width)]
where the time goes in v3:
time: 87.9 us; the launch traced here: 87.7 us
  Pallas kernels  86.9 us (99%)
    pallas_call x1, Pallas kernels, per_device(): pl.pallas_call(functools.partial(kernel, (experts, rows, width, lot)), ou...  83.2 us
    pallas_call x1, Pallas kernels, per_device(): pl.pallas_call(store, out_shape=tuple((jax.ShapeDtypeStruct(r.shape, r.dt...  3.79 us

profile of v3, /device:TPU:0, one launch (start us, length us, event | category | flops | bytes accessed | tf_op | source)
XLA Modules:
  0.0 87.7 jit_solution(2932521658776351713)
XLA Ops:
  0.6 83.2 %cross_experts.1 = (bf16[256,512]{1,0:T(8,128)(2,1)S(1)}, bf16[256,2,512]{2,1,0:T(2,128)(2,1)S(1)}, bf16[256,512]{1,0:T(8,128)(2,1)S(1)}, bf16[1024,4096]{1,0:T(8,128)(2,1)S(1)}, f32[1,512]{1,0:T(1,128)S(1)}) custom-call(bf16[256,2,512]{2,1,0:T(2,128)(2,1)} %x_ref.1, bf16[256,512]{1,0:T(8,128)(2,1)} %base_ref.1, bf16[256,512]{1,0:T(8,128)(2,1)} %cot_ref.1, ...), custom_call_target="tpu_custom_call" | custom-call | tf_op jit(solution)/shard_map/cross_experts/pallas_call | solution.py:370
  83.8 3.8 %store.1 = (bf16[256,512]{1,0:T(8,128)(2,1)}, bf16[256,2,512]{2,1,0:T(2,128)(2,1)}, bf16[256,512]{1,0:T(8,128)(2,1)}, bf16[1024,4096]{1,0:T(8,128)(2,1)}, f32[1,512]{1,0:T(1,128)}) custom-call(bf16[256,512]{1,0:T(8,128)(2,1)S(1)} %get-tuple-element.15.refs_0_, bf16[256,2,512]{2,1,0:T(2,128)(2,1)S(1)} %get-tuple-element.16.refs_1_, ...), custom_call_target="tpu_custom_call" | custom-call | tf_op jit(solution)/shard_map/store/pallas_call | solution.py:411
